TPU v7x, 768 devices: a whole 4x8x12 slice. The times are simulated.
768 devices in a mesh: dp: 64 (over z_lo, y, core), section: 12 (over x, z_hi).
Axes of the slice: x: 4, y: 8, z: 12 (z_hi: 3, z_lo: 4; z = z_hi * 4 + z_lo), core: 2. Of those that a mesh axis runs over, the one named last changes fastest.
Arguments:
- saved_inputs: bfloat16 [12, 64, 2, 384, 2048], P('section', 'dp'), may hold values from -16 to 16
- hidden_grads: bfloat16 [12, 64, 2, 384, 256], P('section', 'dp'), may hold values from -0.029907227 to 0.029907227
- block_expert: int32 [12, 64, 2, 3], P('section', 'dp'), may hold values from 0 to 1, as said below
- live_counts: int32 [12, 64, 2, 2], P('section', 'dp'), may hold values from 0 to 384, as said below
- first_moment: float32 [12, 2048, 2, 256], P('section', 'dp'), may hold values from -3 to 3
- second_moment: float32 [12, 2048, 2, 256], P('section', 'dp'), may hold values from 0.05 to 2
Outputs:
- grad_total: float32 [12, 2048, 2, 256], P('section', 'dp')
- new_first: float32 [12, 2048, 2, 256], P('section', 'dp')
- new_second: float32 [12, 2048, 2, 256], P('section', 'dp')
- step_direction: float32 [12, 2048, 2, 256], P('section', 'dp')
Inputs may be any that keep to these rules, and one draw needn't show every extreme that they name: block_expert[p, d, k, b] names the expert of rows b * 128 to (b + 1) * 128 - 1 of that device's direction-k rows. live_counts[p, d, k, e] is 0 when no block of that direction names expert e; for n such blocks it lies between 128 * (n - 1) + 1 and 128 * n. On every device one of the two directions has all its blocks on one expert with all 384 rows live.
All inputs are finite; a program needn't handle non-finite values.
Results may differ from a plain program's by a relative error of at most 0.0021.
Values may be sent and summed in bfloat16 or wider, within the bound.
A program may use at most 64 MiB of HBM per device.

v0:
```python
import jax
import jax.numpy as jnp
from jax import lax
from jax.sharding import PartitionSpec as P

EXPERTS = 2
BLOCK = 128
NBLK = 3


beta_one = 0.9
beta_two = 0.95
adam_epsilon = 1e-08
bias_first = 1.0 - 0.9**50
bias_second = 1.0 - 0.95**50


def shifted(value, axis, steps):
    count = lax.axis_size(axis)
    pairs = [(source, (source + steps) % count) for source in range(count)]
    return lax.ppermute(value, axis, pairs)


def route_select(block_expert, live_counts):
    experts = jnp.arange(EXPERTS, dtype=jnp.int32)
    onehot = (block_expert[..., :, None] == experts).astype(jnp.int32)
    earlier = jnp.cumsum(onehot, axis=-2) - onehot
    before = jnp.sum(earlier * onehot, axis=-1)
    limits = jnp.sum(live_counts[..., None, :] * onehot, axis=-1)
    offsets = jnp.arange(BLOCK, dtype=jnp.int32)
    positions = before[..., None] * BLOCK + offsets
    live_rows = positions < limits[..., None]
    return (live_rows, onehot)


def per_device(saved_inputs, hidden_grads, block_expert, live_counts, first_moment, second_moment):
    model_width = saved_inputs.shape[4]
    hidden = hidden_grads.shape[4]
    live_rows, onehot = route_select(block_expert.reshape(2, NBLK), live_counts.reshape(2, EXPERTS))
    weights = onehot.astype(jnp.float32)
    inputs = saved_inputs.reshape(2, NBLK, BLOCK, model_width)
    masked = hidden_grads.reshape(2, NBLK, BLOCK, hidden) * live_rows[..., None].astype(
        jnp.bfloat16
    )
    half_span = lax.axis_size("section") // 2

    def direction_part(direction):
        columns = inputs[direction]
        blocks = jnp.einsum(
            "brd,brf->bdf", columns, masked[direction], preferred_element_type=jnp.float32
        )
        return jnp.einsum(
            "bdf,be->def", blocks, weights[direction], precision=lax.Precision.HIGHEST
        )

    sent_part = direction_part(1).astype(jnp.bfloat16)
    partner = shifted(sent_part, "section", half_span).astype(jnp.float32)
    grad_total = lax.psum_scatter(
        direction_part(0) + partner, "dp", scatter_dimension=0, tiled=True
    )
    moment_one = first_moment[0]
    moment_two = second_moment[0]
    new_first = beta_one * moment_one + (1.0 - beta_one) * grad_total
    new_second = beta_two * moment_two + (1.0 - beta_two) * grad_total * grad_total
    step_direction = new_first / bias_first / (jnp.sqrt(new_second / bias_second) + adam_epsilon)
    return (grad_total[None], new_first[None], new_second[None], step_direction[None])


def solution(mesh):
    in_specs = (
        P("section", "dp", None, None, None),
        P("section", "dp", None, None, None),
        P("section", "dp", None, None),
        P("section", "dp", None, None),
        P("section", "dp", None, None),
        P("section", "dp", None, None),
    )
    out_specs = (
        P("section", "dp", None, None),
        P("section", "dp", None, None),
        P("section", "dp", None, None),
        P("section", "dp", None, None),
    )
    return jax.shard_map(
        per_device, mesh=mesh, in_specs=in_specs, out_specs=out_specs, check_vma=False
    )
```

profile of v0, /device:TPU:1, one launch (start us, length us, event | category | flops | bytes accessed | tf_op | source)
XLA Modules:
  0.0 687.4 jit_solution(3223904086986463222)
XLA Ops:
  7.2 0.0 copy-start
  7.2 0.0 all-reduce.3.cloned.1.call-start
  7.2 0.7 fusion.18
  7.9 0.3 reduce_window_sum.11
  8.3 0.8 select_reduce_fusion.1
  9.1 2.2 fusion.21
  11.3 0.1 fusion.16
  11.4 0.0 copy-done
  11.4 0.2 broadcast_multiply_fusion
  11.5 3.7 fusion.12
  15.3 9.1 %copy.11 = f32[3,256,2048]{1,0,2:T(4,128)} copy(f32[3,256,2048]{2,1,0:T(8,128)} %fusion.12) | data formatting | bytes 12582912 | tf_op jit(solution)/shard_map/brd,brf->bdf/dot_general | solution.py:49
  24.3 18.2 %fusion.9 = bf16[2048,2,256]{2,1,0:T(2,128)(2,1)} fusion(f32[3,256,2048]{1,0,2:T(4,128)} %copy.11, f32[2,3,2]{1,2,0:T(2,128)S(1)} %get-tuple-element.12), kind=kOutput, calls=%fused_computation.6 | convolution fusion | flops 38797312 | bytes 8389632 | tf_op jit(solution)/shard_map/bdf,be->def/dot_general | solution.py:52
  42.5 5.6 collective-permute-start
  48.2 3.7 fusion.13
  51.9 9.1 %copy.10 = f32[3,256,2048]{1,0,2:T(4,128)} copy(f32[3,256,2048]{2,1,0:T(8,128)} %fusion.13) | data formatting | bytes 12582912 | tf_op jit(solution)/shard_map/brd,brf->bdf/dot_general | solution.py:49
  61.0 25.6 %collective-permute-done = bf16[2048,2,256]{2,1,0:T(2,128)(2,1)} collective-permute-done((bf16[2048,2,256]{2,1,0:T(2,128)(2,1)}, bf16[2048,2,256]{2,1,0:T(2,128)(2,1)}, u32[]{:S(2)}, u32[]{:S(2)}) %collective-permute-start) | collective-permute-done | bytes 2097184 | tf_op jit(solution)/shard_map/ppermute | solution.py:21
  86.6 19.7 %bitcast_add_fusion = f32[2048,2,256]{2,1,0:T(2,128)} fusion(bf16[2048,2,256]{2,1,0:T(2,128)(2,1)} %collective-permute-done, f32[3,256,2048]{1,0,2:T(4,128)} %copy.10, f32[2,3,2]{1,2,0:T(2,128)S(1)} %get-tuple-element.12), kind=kOutput, calls=%fused_computation.4 | convolution fusion | flops 39845888 | bytes 12583936 | tf_op jit(solution)/shard_map/bdf,be->def/dot_general | solution.py:52
  106.4 0.0 copy-start.1
  106.4 0.0 copy-start.2
  106.4 0.0 all-reduce.3.cloned.1.call-update
  106.4 1.3 dynamic-slice
  108.4 570.5 %all-reduce.3.cloned.1.call-done = f32[2048,2,256]{2,1,0:T(2,128)} async-done(((f32[2048,2,256]{2,1,0:T(2,128)}), f32[2048,2,256]{2,1,0:T(2,128)}) %all-reduce.3.cloned.1.call-update) | async-done | bytes 4194320
  678.8 0.0 copy-done.1
  678.8 0.0 copy-done.2
  678.8 1.7 fusion.15
  (1 shorter events, 0.0 us)
Async XLA Ops:
  7.2 4.2 copy-start
  7.2 671.6 %all-reduce.3.cloned.1.call-start = ((), (), s32[]{:S(2)}) async-start(), calls=%async_computation | async-start | bytes 8388608
  42.5 44.1 %collective-permute-start = (bf16[2048,2,256]{2,1,0:T(2,128)(2,1)}, bf16[2048,2,256]{2,1,0:T(2,128)(2,1)}, u32[]{:S(2)}, u32[]{:S(2)}) collective-permute-start(bf16[2048,2,256]{2,1,0:T(2,128)(2,1)} %fusion.9), channel_id=1, source_target_pairs={{0,6},{1,7},{2,8},{3,9},{4,10},{5,11},{6,0},{7,1},{8,2},{9,3},{10,... | collective-permute-start | bytes 6291464 | tf_op jit(solution)/shard_map/ppermute | solution.py:21
  106.4 572.5 %copy-start.1 = (f32[1,32,2,256]{3,2,1,0:T(2,128)S(1)}, f32[1,32,2,256]{3,2,1,0:T(2,128)}, u32[]{:S(2)}) copy-start(f32[1,32,2,256]{3,2,1,0:T(2,128)} %param.10) | copy-start | bytes 196612
  106.4 572.5 %copy-start.2 = (f32[1,32,2,256]{3,2,1,0:T(2,128)S(1)}, f32[1,32,2,256]{3,2,1,0:T(2,128)}, u32[]{:S(2)}) copy-start(f32[1,32,2,256]{3,2,1,0:T(2,128)} %param.11) | copy-start | bytes 196612
Sparse Core Ops, SparseCore 0:
  106.5 572.2 all-reduce.2
where the time goes:
time: 688 us; the launch traced here: 687 us
  waiting for transfers between devices  596 us (87%)
  matrix products  45.4 us (7%)
  local copies, waits for them, and re-layouts  21.7 us (3%)
  between operations  14.7 us (2%)
    unnamed x2, waiting for transfers between devices  570 us
    dot_general x2, matrix products, direction_part(): jnp.einsum('bdf,be->def', blocks, weights[direction], precision=lax.Preci...  37.9 us
    ppermute x1, waiting for transfers between devices, shifted(): return lax.ppermute(value, axis, pairs)  25.6 us
    dot_general x2, local copies, waits for them, and re-layouts, direction_part(): jnp.einsum('brd,brf->bdf', columns, masked[direction], preferred_element_...  18.2 us
  transfers between devices with their start and end apart: 2, of which 2 were waited for; matrix products, arithmetic and copies ran while one was open for 2% of the time, Pallas kernels for 0%

commit v1 on v0

v1 whole, which is shorter than its diff:
```python
import functools

import jax
import jax.numpy as jnp
from jax import lax
from jax.experimental import pallas as pl
from jax.experimental.pallas import tpu as pltpu
from jax.sharding import PartitionSpec as P

MESH = pl.DeviceIdType.MESH
EXPERTS = 2
BLOCK = 128
NBLK = 3
ROWS = BLOCK * NBLK
D = 2048
FF = 256
WIDE = EXPERTS * FF
HALF = D // 2
YS = 8
ZS = 4

beta_one = 0.9
beta_two = 0.95
adam_epsilon = 1e-08
bias_first = 1.0 - 0.9**50
bias_second = 1.0 - 0.95**50


def kernel(
    be_ref, lc_ref, x_hbm, g_hbm, low_ref, high_ref,
    xb, graw, gb, total, mirror_out, mirror_in, ring_a, ring_b, last, zbuf,
    load_sem, pair_send, pair_recv, mir_send, mir_recv,
    a_send, a_recv, b_send, b_recv, z_send, z_recv,
):
    dp = lax.axis_index("dp")
    sec = lax.axis_index("section")
    core = dp % 2
    y = (dp // 2) % YS
    z = dp // (2 * YS)
    sgn = 1 - 2 * core

    def at(zz, yy, cc):
        return {"dp": zz * (2 * YS) + yy * 2 + cc, "section": sec}

    partner = at(z, y, 1 - core)
    mirror = {"dp": dp, "section": (sec + 6) % 12}
    next_a = at(z, (y + sgn + YS) % YS, core)
    next_b = at(z, (y - sgn + YS) % YS, core)

    def remote(src, dst, send, recv, device):
        return pltpu.make_async_remote_copy(
            src_ref=src, dst_ref=dst, send_sem=send, recv_sem=recv, device_id=device, device_id_type=MESH
        )

    mine = pl.ds(pl.multiple_of(core * HALF, HALF), HALF)
    other = pl.ds(pl.multiple_of((1 - core) * HALF, HALF), HALF)
    load_g = pltpu.make_async_copy(g_hbm, graw, load_sem.at[2])
    load_g.start()
    loads = [pltpu.make_async_copy(x_hbm.at[k, :, mine], xb.at[0, k], load_sem.at[k]) for k in range(2)]
    loads[1].start()
    loads[0].start()

    barrier = pltpu.get_barrier_semaphore()
    peers = [partner, mirror, next_a, next_b]
    for dz in range(1, ZS):
        for cc in range(2):
            peers.append(at((z + dz) % ZS, y, cc))
    for peer in peers:
        pl.semaphore_signal(barrier, inc=1, device_id=peer, device_id_type=MESH)

    load_g.wait()
    rows = lax.broadcasted_iota(jnp.int32, (BLOCK, FF), 0)

    def mask_direction(k):
        for b in range(NBLK):
            owner = be_ref[k, b]
            before = jnp.int32(0)
            for c in range(b):
                before = before + jnp.where(be_ref[k, c] == owner, BLOCK, 0)
            block = graw[k, pl.ds(b * BLOCK, BLOCK), :].astype(jnp.float32)
            for e in range(EXPERTS):
                limit = jnp.where(owner == e, lc_ref[k, e], 0) - before
                kept = jnp.where(rows < limit, block, 0.0).astype(jnp.bfloat16)
                gb[0, k, pl.ds(b * BLOCK, BLOCK), pl.ds(e * FF, FF)] = kept

    mask_direction(1)
    mask_direction(0)
    pl.semaphore_wait(barrier, len(peers))

    send_x = [remote(x_hbm.at[k, :, other], xb.at[1, k], pair_send.at[k], pair_recv.at[k], partner) for k in range(2)]
    send_g = [remote(gb.at[0, k], gb.at[1, k], pair_send.at[2 + k], pair_recv.at[2 + k], partner) for k in range(2)]
    for k in (1, 0):
        send_g[k].start()
        send_x[k].start()

    def off(d):
        return (y + sgn * d + YS) % YS

    first_pair = off(4) // 2

    def tile(k, t, pair):
        columns = pl.ds(pl.multiple_of(t * (HALF // 2) + pair * 128, 128), 128)
        acc = None
        for who in range(2):
            part = lax.dot_general(
                xb[who, k, :, columns],
                gb[who, k],
                (((0,), (0,)), ((), ())),
                preferred_element_type=jnp.float32,
            )
            acc = part if acc is None else acc + part
        return acc

    def mirror_tiles(order):
        n = len(order)

        def body(i, carry):
            t = i % 2
            step = i // 2
            shift = order[0] if n == 1 else jnp.where(step == 0, order[0], order[1])
            pair = (first_pair + shift) % 4
            value = tile(1, t, pair).astype(jnp.bfloat16)
            mirror_out[2 * pair, t] = value[:64]
            mirror_out[2 * pair + 1, t] = value[64:]
            return carry

        lax.fori_loop(0, 2 * n, body, 0)

    def send_mirror(d, slot):
        v = off(d)
        copy = remote(mirror_out.at[v], mirror_in.at[v], mir_send.at[slot], mir_recv.at[slot], mirror)
        copy.start()
        return copy

    loads[1].wait()
    send_g[1].wait_recv()
    send_x[1].wait_recv()
    mirrors = {}
    mirror_tiles([0])
    mirrors[4] = send_mirror(4, 0)
    mirror_tiles([1, 3])
    for slot, d in enumerate((3, -3, 2, -2)):
        mirrors[d] = send_mirror(d, 1 + slot)
    mirror_tiles([2])
    for slot, d in enumerate((1, -1, 0)):
        mirrors[d] = send_mirror(d, 5 + slot)

    loads[0].wait()
    send_g[0].wait_recv()
    send_x[0].wait_recv()

    def own_body(i, carry):
        t = i % 2
        pair = (first_pair + i // 2) % 4
        value = tile(0, t, pair)
        total[2 * pair, t] = value[:64]
        total[2 * pair + 1, t] = value[64:]
        return carry

    lax.fori_loop(0, 8, own_body, 0)

    def add_mirror(d):
        v = off(d)
        mirrors[d].wait_recv()
        total[v] = total[v] + mirror_in[v].astype(jnp.float32)

    sends = []

    def start(src, dst, send, recv, device):
        copy = remote(src, dst, send, recv, device)
        copy.start()
        sends.append(copy)

    def got(ring, sems, ssems, step, t, device):
        remote(ring.at[step, t], ring.at[step, t], ssems.at[step, t], sems.at[step, t], device).wait_recv()

    def forward_a(step, d):
        for t in range(2):
            got(ring_a, a_recv, a_send, step, t, next_a)
            ring_a[step, t] = ring_a[step, t] + total[off(d), t]
            start(ring_a.at[step, t], ring_a.at[step + 1, t], a_send.at[step + 1, t], a_recv.at[step + 1, t], next_a)

    def forward_b(step, d):
        for t in range(2):
            got(ring_b, b_recv, b_send, step, t, next_b)
            ring_b[step, t] = ring_b[step, t] + total[off(d), t]
            start(ring_b.at[step, t], ring_b.at[step + 1, t], b_send.at[step + 1, t], b_recv.at[step + 1, t], next_b)

    add_mirror(4)
    for t in range(2):
        start(total.at[off(4), t], ring_a.at[0, t], a_send.at[0, t], a_recv.at[0, t], next_a)
    add_mirror(3)
    forward_a(0, 3)
    add_mirror(-3)
    for t in range(2):
        start(total.at[off(-3), t], ring_b.at[0, t], b_send.at[0, t], b_recv.at[0, t], next_b)
    add_mirror(2)
    forward_a(1, 2)
    add_mirror(-2)
    forward_b(0, -2)
    add_mirror(1)
    forward_a(2, 1)
    add_mirror(-1)
    forward_b(1, -1)
    add_mirror(0)

    def z_copy(t, k):
        zt = 2 * core + t
        return remote(
            last.at[t, pl.ds(32 * k, 32)], zbuf.at[z], z_send.at[t, k], z_recv.at[z], at(zt, y, k)
        )

    def is_self(t, k):
        return jnp.logical_and(2 * core + t == z, core == k)

    for t in range(2):
        got(ring_a, a_recv, a_send, 3, t, next_a)
        got(ring_b, b_recv, b_send, 2, t, next_b)
        last[t] = total[y, t] + (ring_a[3, t] + ring_b[2, t])
        for k in range(2):

            @pl.when(jnp.logical_not(is_self(t, k)))
            def _():
                z_copy(t, k).start()

            @pl.when(is_self(t, k))
            def _():
                zbuf[z] = last[t, pl.ds(32 * k, 32)]

    def z_wait(source):
        remote(zbuf.at[source], zbuf.at[source], z_send.at[0, 0], z_recv.at[source], partner).wait_recv()

    for dz in range(1, ZS):
        z_wait((z + dz) % ZS)

    @pl.when(core != z // 2)
    def _():
        z_wait(z)

    for i, out_ref in enumerate((low_ref, high_ref)):
        result = zbuf[2 * i] + zbuf[2 * i + 1]
        for e in range(EXPERTS):
            out_ref[:, e, :] = result[:, e * FF : (e + 1) * FF]

    for k in range(2):
        send_x[k].wait_send()
        send_g[k].wait_send()
    for copy in mirrors.values():
        copy.wait_send()
    for copy in sends:
        copy.wait_send()
    for t in range(2):
        for k in range(2):

            @pl.when(jnp.logical_not(is_self(t, k)))
            def _():
                z_copy(t, k).wait_send()


def per_device(saved_inputs, hidden_grads, block_expert, live_counts, first_moment, second_moment):
    any_spec = pl.BlockSpec(memory_space=pl.ANY)
    smem_spec = pl.BlockSpec(memory_space=pltpu.SMEM)
    low, high = pl.pallas_call(
        kernel,
        out_shape=[jax.ShapeDtypeStruct((32, EXPERTS, FF), jnp.float32)] * 2,
        in_specs=[smem_spec, smem_spec, any_spec, any_spec],
        out_specs=[pl.BlockSpec(memory_space=pltpu.VMEM)] * 2,
        scratch_shapes=[
            pltpu.VMEM((2, 2, ROWS, HALF), jnp.bfloat16),
            pltpu.VMEM((2, ROWS, FF), jnp.bfloat16),
            pltpu.VMEM((2, 2, ROWS, WIDE), jnp.bfloat16),
            pltpu.VMEM((YS, 2, 64, WIDE), jnp.float32),
            pltpu.VMEM((YS, 2, 64, WIDE), jnp.bfloat16),
            pltpu.VMEM((YS, 2, 64, WIDE), jnp.bfloat16),
            pltpu.VMEM((4, 2, 64, WIDE), jnp.float32),
            pltpu.VMEM((3, 2, 64, WIDE), jnp.float32),
            pltpu.VMEM((2, 64, WIDE), jnp.float32),
            pltpu.VMEM((ZS, 32, WIDE), jnp.float32),
            pltpu.SemaphoreType.DMA((3,)),
            pltpu.SemaphoreType.DMA((4,)),
            pltpu.SemaphoreType.DMA((4,)),
            pltpu.SemaphoreType.DMA((8,)),
            pltpu.SemaphoreType.DMA((8,)),
            pltpu.SemaphoreType.DMA((4, 2)),
            pltpu.SemaphoreType.DMA((4, 2)),
            pltpu.SemaphoreType.DMA((3, 2)),
            pltpu.SemaphoreType.DMA((3, 2)),
            pltpu.SemaphoreType.DMA((2, 2)),
            pltpu.SemaphoreType.DMA((ZS,)),
        ],
        compiler_params=pltpu.CompilerParams(
            collective_id=0, has_side_effects=True, vmem_limit_bytes=66700000
        ),
    )(
        block_expert.reshape(2, NBLK),
        live_counts.reshape(2, EXPERTS),
        saved_inputs.reshape(2, ROWS, D),
        hidden_grads.reshape(2, ROWS, FF),
    )
    grad_total = low + high
    moment_one = first_moment[0]
    moment_two = second_moment[0]
    new_first = beta_one * moment_one + (1.0 - beta_one) * grad_total
    new_second = beta_two * moment_two + (1.0 - beta_two) * grad_total * grad_total
    step_direction = new_first / bias_first / (jnp.sqrt(new_second / bias_second) + adam_epsilon)
    return (grad_total[None], new_first[None], new_second[None], step_direction[None])


def solution(mesh):
    in_specs = (
        P("section", "dp", None, None, None),
        P("section", "dp", None, None, None),
        P("section", "dp", None, None),
        P("section", "dp", None, None),
        P("section", "dp", None, None),
        P("section", "dp", None, None),
    )
    out_specs = (
        P("section", "dp", None, None),
        P("section", "dp", None, None),
        P("section", "dp", None, None),
        P("section", "dp", None, None),
    )
    return jax.shard_map(
        per_device, mesh=mesh, in_specs=in_specs, out_specs=out_specs, check_vma=False
    )
```

time: 688 us -> 53.2 us (0.08)
  waiting for transfers between devices: 596 us -> 0 us
  Pallas kernels: 0 us -> 49.8 us
  matrix products: 45.4 us -> 0 us
  local copies, waits for them, and re-layouts: 21.7 us -> 0.01 us
  between operations: 14.7 us -> 0.67 us
    unnamed x2 -> x0, waiting for transfers between devices: 570 us -> none
    pallas_call x0 -> x1, Pallas kernels: none -> 49.8 us  [per_device(): pl.pallas_call(kernel, out_shape=[jax.ShapeDtypeStruct((32, EXPERTS, FF),...]
    dot_general x4 -> x0, matrix products: 45.4 us -> none  [the longest x2 37.9 us: direction_part(): jnp.einsum('bdf,be->def', blocks, weights[direction], precision=lax.Preci...]
    ppermute x1 -> x0, waiting for transfers between devices: 25.6 us -> none  [shifted(): return lax.ppermute(value, axis, pairs)]
    dot_general x2 -> x0, local copies, waits for them, and re-layouts: 18.2 us -> none  [direction_part(): jnp.einsum('brd,brf->bdf', columns, masked[direction], preferred_element_...]
  transfers between devices with their start and end apart: 2 -> 0, of which waited for: 2 -> 0; matrix products, arithmetic and copies ran while one was open for 2% -> 0% of each run, Pallas kernels for 0% -> 0%
where the time goes in v1:
time: 53.2 us; the launch traced here: 53 us
  Pallas kernels  49.8 us (94%)
  other arithmetic  2.45 us (5%)
  between operations  0.67 us (1%)
    pallas_call x1, Pallas kernels, per_device(): pl.pallas_call(kernel, out_shape=[jax.ShapeDtypeStruct((32, EXPERTS, FF),...  49.8 us
    broadcast_in_dim x1, other arithmetic, per_device(): step_direction[None]  1.69 us

profile of v1, /device:TPU:1, one launch (start us, length us, event | category | flops | bytes accessed | tf_op | source)
XLA Modules:
  0.0 53.0 jit_solution(13610220776460740579)
XLA Ops:
  0.6 0.0 copy-start.1
  0.6 0.0 copy-start
  0.7 49.8 %shard_map.93 = (f32[32,2,256]{2,1,0:T(2,128)}, f32[32,2,256]{2,1,0:T(2,128)}) custom-call(s32[2,3]{1,0:T(2,128)} %bitcast.26, s32[2,2]{1,0:T(2,128)} %bitcast.27, bf16[2,384,2048]{2,1,0:T(8,128)(2,1)} %bitcast.23, bf16[2,384,256]{2,1,0:T(8,128)(2,1)} %bitcast.24), custom_call_target="tpu_custom_call" | custom-call | tf_op jit(solution)/shard_map/pallas_call | solution.py:263
  50.5 0.0 copy-done.1
  50.5 0.0 copy-done
  50.5 1.7 %fusion.1 = (f32[1,32,2,256]{3,2,1,0:T(2,128)}, f32[32,2,256]{2,1,0:T(2,128)S(1)}) fusion(f32[1,32,2,256]{3,2,1,0:T(2,128)S(1)} %copy-done, f32[1,32,2,256]{3,2,1,0:T(2,128)S(1)} %copy-done.1, f32[32,2,256]{2,1,0:T(2,128)} %get-tuple-element.6, f32[32,2,256]{2,1,0:T(2,128)} %get-tuple-element.7), kind=kLoop, calls=%fused_computation.4 | loop fusion | flops 196608 | bytes 393216 | tf_op jit(solution)/shard_map/broadcast_in_dim | solution.py:306
  52.2 0.0 copy-start.2
  52.2 0.8 %fusion.3 = (f32[1,32,2,256]{3,2,1,0:T(2,128)}, f32[1,32,2,256]{3,2,1,0:T(2,128)}) fusion(f32[32,2,256]{2,1,0:T(2,128)S(1)} %get-tuple-element.9, f32[1,32,2,256]{3,2,1,0:T(2,128)S(1)} %copy-done.1, f32[1,32,2,256]{3,2,1,0:T(2,128)S(1)} %copy-done), kind=kLoop, calls=%fused_computation.6 | loop fusion | flops 114688 | bytes 327680 | tf_op jit(solution)/shard_map/broadcast_in_dim | solution.py:306
  53.0 0.0 copy-done.2
Async XLA Ops:
  0.6 49.9 %copy-start.1 = (f32[1,32,2,256]{3,2,1,0:T(2,128)S(1)}, f32[1,32,2,256]{3,2,1,0:T(2,128)}, u32[]{:S(2)}) copy-start(f32[1,32,2,256]{3,2,1,0:T(2,128)} %param.11) | copy-start | bytes 196612
  0.6 49.9 %copy-start = (f32[1,32,2,256]{3,2,1,0:T(2,128)S(1)}, f32[1,32,2,256]{3,2,1,0:T(2,128)}, u32[]{:S(2)}) copy-start(f32[1,32,2,256]{3,2,1,0:T(2,128)} %param.10) | copy-start | bytes 196612
  52.2 0.8 %copy-start.2 = (f32[32,2,256]{2,1,0:T(2,128)}, f32[32,2,256]{2,1,0:T(2,128)S(1)}, u32[]{:S(2)}) copy-start(f32[32,2,256]{2,1,0:T(2,128)S(1)} %get-tuple-element.9) | copy-start | bytes 196612

commit v2 on v1

--- a/solution.py
+++ b/solution.py
@@ -29,7 +29,7 @@
 def kernel(
     be_ref, lc_ref, x_hbm, g_hbm, low_ref, high_ref,
     xb, graw, gb, total, mirror_out, mirror_in, ring_a, ring_b, last, zbuf,
-    load_sem, pair_send, pair_recv, mir_send, mir_recv,
+    load_sem, tile_send, tile_recv, pair_send, pair_recv, mir_send, mir_recv,
     a_send, a_recv, b_send, b_recv, z_send, z_recv,
 ):
     dp = lax.axis_index("dp")
@@ -68,7 +68,29 @@
     for peer in peers:
         pl.semaphore_signal(barrier, inc=1, device_id=peer, device_id_type=MESH)
 
-    load_g.wait()
+    def off(d):
+        return (y + sgn * d + YS) % YS
+
+    first_pair = off(4) // 2
+    shifts = (0, 1, 3, 2)
+
+    def columns_of(pair, t, half):
+        return pl.ds(pl.multiple_of(half * HALF + t * (HALF // 2) + pair * 128, 128), 128)
+
+    def tile_copy(i, shift, t):
+        pair = (first_pair + shift) % 4
+        return remote(
+            x_hbm.at[1, :, columns_of(pair, t, 1 - core)],
+            xb.at[1, 1, :, columns_of(pair, t, 0)],
+            tile_send.at[i],
+            tile_recv.at[i],
+            partner,
+        )
+
+    tiles = [tile_copy(2 * i + t, shift, t) for i, shift in enumerate(shifts) for t in range(2)]
+    send_x = remote(x_hbm.at[0, :, other], xb.at[1, 0], pair_send.at[2], pair_recv.at[2], partner)
+    send_g = [remote(gb.at[0, k], gb.at[1, k], pair_send.at[k], pair_recv.at[k], partner) for k in range(2)]
+
     rows = lax.broadcasted_iota(jnp.int32, (BLOCK, FF), 0)
 
     def mask_direction(k):
@@ -83,20 +105,17 @@
                 kept = jnp.where(rows < limit, block, 0.0).astype(jnp.bfloat16)
                 gb[0, k, pl.ds(b * BLOCK, BLOCK), pl.ds(e * FF, FF)] = kept
 
+    pl.semaphore_wait(barrier, len(peers))
+    for copy in tiles[:2]:
+        copy.start()
+    load_g.wait()
     mask_direction(1)
+    send_g[1].start()
+    for copy in tiles[2:]:
+        copy.start()
     mask_direction(0)
-    pl.semaphore_wait(barrier, len(peers))
-
-    send_x = [remote(x_hbm.at[k, :, other], xb.at[1, k], pair_send.at[k], pair_recv.at[k], partner) for k in range(2)]
-    send_g = [remote(gb.at[0, k], gb.at[1, k], pair_send.at[2 + k], pair_recv.at[2 + k], partner) for k in range(2)]
-    for k in (1, 0):
-        send_g[k].start()
-        send_x[k].start()
-
-    def off(d):
-        return (y + sgn * d + YS) % YS
-
-    first_pair = off(4) // 2
+    send_g[0].start()
+    send_x.start()
 
     def tile(k, t, pair):
         columns = pl.ds(pl.multiple_of(t * (HALF // 2) + pair * 128, 128), 128)
@@ -111,58 +130,74 @@
             acc = part if acc is None else acc + part
         return acc
 
-    def mirror_tiles(order):
-        n = len(order)
-
+    def mirror_tiles(first, count):
         def body(i, carry):
             t = i % 2
             step = i // 2
-            shift = order[0] if n == 1 else jnp.where(step == 0, order[0], order[1])
+            shift = jnp.where(step < 2, step, 5 - step)
             pair = (first_pair + shift) % 4
+            arrived = xb.at[1, 1, :, columns_of(pair, t, 0)]
+            remote(arrived, arrived, tile_send.at[i], tile_recv.at[i], partner).wait_recv()
             value = tile(1, t, pair).astype(jnp.bfloat16)
             mirror_out[2 * pair, t] = value[:64]
             mirror_out[2 * pair + 1, t] = value[64:]
             return carry
 
-        lax.fori_loop(0, 2 * n, body, 0)
-
-    def send_mirror(d, slot):
+        lax.fori_loop(2 * first, 2 * (first + count), body, 0)
+
+    pieces = [(t, k) for t in range(2) for k in range(2)]
+    mirrors = {}
+
+    def rows_of(k):
+        return pl.ds(32 * k, 32)
+
+    def send_mirror(d, t, k):
         v = off(d)
-        copy = remote(mirror_out.at[v], mirror_in.at[v], mir_send.at[slot], mir_recv.at[slot], mirror)
+        copy = remote(
+            mirror_out.at[v, t, rows_of(k)],
+            mirror_in.at[v, t, rows_of(k)],
+            mir_send.at[d + 3, 2 * t + k],
+            mir_recv.at[d + 3, 2 * t + k],
+            mirror,
+        )
         copy.start()
-        return copy
+        mirrors[d, t, k] = copy
+
+    def own_tiles(first, count):
+        def body(i, carry):
+            t = i % 2
+            step = i // 2
+            shift = jnp.where(step < 2, step, 5 - step)
+            pair = (first_pair + shift) % 4
+            value = tile(0, t, pair)
+            total[2 * pair, t] = value[:64]
+            total[2 * pair + 1, t] = value[64:]
+            return carry
+
+        lax.fori_loop(2 * first, 2 * (first + count), body, 0)
 
     loads[1].wait()
     send_g[1].wait_recv()
-    send_x[1].wait_recv()
-    mirrors = {}
-    mirror_tiles([0])
-    mirrors[4] = send_mirror(4, 0)
-    mirror_tiles([1, 3])
-    for slot, d in enumerate((3, -3, 2, -2)):
-        mirrors[d] = send_mirror(d, 1 + slot)
-    mirror_tiles([2])
-    for slot, d in enumerate((1, -1, 0)):
-        mirrors[d] = send_mirror(d, 5 + slot)
-
+    mirror_tiles(0, 1)
+    for t, k in pieces:
+        send_mirror(4, t, k)
+    mirror_tiles(1, 2)
+    for t, k in pieces:
+        send_mirror(-3, t, k)
+    for t, k in pieces:
+        send_mirror(3, t, k)
+    for t, k in pieces:
+        send_mirror(2, t, k)
+        send_mirror(-2, t, k)
     loads[0].wait()
     send_g[0].wait_recv()
-    send_x[0].wait_recv()
-
-    def own_body(i, carry):
-        t = i % 2
-        pair = (first_pair + i // 2) % 4
-        value = tile(0, t, pair)
-        total[2 * pair, t] = value[:64]
-        total[2 * pair + 1, t] = value[64:]
-        return carry
-
-    lax.fori_loop(0, 8, own_body, 0)
-
-    def add_mirror(d):
+    send_x.wait_recv()
+    own_tiles(0, 3)
+
+    def add_mirror(d, t, k):
         v = off(d)
-        mirrors[d].wait_recv()
-        total[v] = total[v] + mirror_in[v].astype(jnp.float32)
+        mirrors[d, t, k].wait_recv()
+        total[v, t, rows_of(k)] = total[v, t, rows_of(k)] + mirror_in[v, t, rows_of(k)].astype(jnp.float32)
 
     sends = []
 
@@ -171,61 +206,72 @@
         copy.start()
         sends.append(copy)
 
-    def got(ring, sems, ssems, step, t, device):
-        remote(ring.at[step, t], ring.at[step, t], ssems.at[step, t], sems.at[step, t], device).wait_recv()
-
-    def forward_a(step, d):
-        for t in range(2):
-            got(ring_a, a_recv, a_send, step, t, next_a)
-            ring_a[step, t] = ring_a[step, t] + total[off(d), t]
-            start(ring_a.at[step, t], ring_a.at[step + 1, t], a_send.at[step + 1, t], a_recv.at[step + 1, t], next_a)
-
-    def forward_b(step, d):
-        for t in range(2):
-            got(ring_b, b_recv, b_send, step, t, next_b)
-            ring_b[step, t] = ring_b[step, t] + total[off(d), t]
-            start(ring_b.at[step, t], ring_b.at[step + 1, t], b_send.at[step + 1, t], b_recv.at[step + 1, t], next_b)
-
-    add_mirror(4)
-    for t in range(2):
-        start(total.at[off(4), t], ring_a.at[0, t], a_send.at[0, t], a_recv.at[0, t], next_a)
-    add_mirror(3)
-    forward_a(0, 3)
-    add_mirror(-3)
-    for t in range(2):
-        start(total.at[off(-3), t], ring_b.at[0, t], b_send.at[0, t], b_recv.at[0, t], next_b)
-    add_mirror(2)
-    forward_a(1, 2)
-    add_mirror(-2)
-    forward_b(0, -2)
-    add_mirror(1)
-    forward_a(2, 1)
-    add_mirror(-1)
-    forward_b(1, -1)
-    add_mirror(0)
+    def got(ring, ssems, sems, step, t, k, device):
+        here = ring.at[step, t, rows_of(k)]
+        remote(here, here, ssems.at[step, 2 * t + k], sems.at[step, 2 * t + k], device).wait_recv()
+
+    def hop(ring, ssems, sems, src, step, t, k, device):
+        p = 2 * t + k
+        start(src, ring.at[step, t, rows_of(k)], ssems.at[step, p], sems.at[step, p], device)
+
+    def forward(ring, ssems, sems, step, d, t, k, device):
+        got(ring, ssems, sems, step, t, k, device)
+        ring[step, t, rows_of(k)] = ring[step, t, rows_of(k)] + total[off(d), t, rows_of(k)]
+        hop(ring, ssems, sems, ring.at[step, t, rows_of(k)], step + 1, t, k, device)
+
+    ways = ((ring_a, a_send, a_recv), (ring_b, b_send, b_recv))
+
+    def forward_a(step, d, t, k):
+        add_mirror(d, t, k)
+        forward(*ways[0], step, d, t, k, next_a)
+
+    def forward_b(step, d, t, k):
+        add_mirror(d, t, k)
+        forward(*ways[1], step, d, t, k, next_b)
+
+    for t, k in pieces:
+        add_mirror(4, t, k)
+        hop(*ways[0], total.at[off(4), t, rows_of(k)], 0, t, k, next_a)
+    mirror_tiles(3, 1)
+    for t, k in pieces:
+        send_mirror(1, t, k)
+        send_mirror(-1, t, k)
+    for t, k in pieces:
+        send_mirror(0, t, k)
+    own_tiles(3, 1)
+    for t, k in pieces:
+        add_mirror(-3, t, k)
+        hop(*ways[1], total.at[off(-3), t, rows_of(k)], 0, t, k, next_b)
+    for t, k in pieces:
+        forward_a(0, 3, t, k)
+    for t, k in pieces:
+        forward_a(1, 2, t, k)
+        forward_b(0, -2, t, k)
+    for t, k in pieces:
+        forward_a(2, 1, t, k)
+        forward_b(1, -1, t, k)
 
     def z_copy(t, k):
         zt = 2 * core + t
-        return remote(
-            last.at[t, pl.ds(32 * k, 32)], zbuf.at[z], z_send.at[t, k], z_recv.at[z], at(zt, y, k)
-        )
+        return remote(last.at[t, rows_of(k)], zbuf.at[z], z_send.at[t, k], z_recv.at[z], at(zt, y, k))
 
     def is_self(t, k):
         return jnp.logical_and(2 * core + t == z, core == k)
 
-    for t in range(2):
-        got(ring_a, a_recv, a_send, 3, t, next_a)
-        got(ring_b, b_recv, b_send, 2, t, next_b)
-        last[t] = total[y, t] + (ring_a[3, t] + ring_b[2, t])
-        for k in range(2):
-
-            @pl.when(jnp.logical_not(is_self(t, k)))
-            def _():
-                z_copy(t, k).start()
-
-            @pl.when(is_self(t, k))
-            def _():
-                zbuf[z] = last[t, pl.ds(32 * k, 32)]
+    for t, k in pieces:
+        add_mirror(0, t, k)
+        got(ring_a, a_send, a_recv, 3, t, k, next_a)
+        got(ring_b, b_send, b_recv, 2, t, k, next_b)
+        part = rows_of(k)
+        last[t, part] = total[y, t, part] + (ring_a[3, t, part] + ring_b[2, t, part])
+
+        @pl.when(jnp.logical_not(is_self(t, k)))
+        def _():
+            z_copy(t, k).start()
+
+        @pl.when(is_self(t, k))
+        def _():
+            zbuf[z] = last[t, part]
 
     def z_wait(source):
         remote(zbuf.at[source], zbuf.at[source], z_send.at[0, 0], z_recv.at[source], partner).wait_recv()
@@ -242,9 +288,8 @@
         for e in range(EXPERTS):
             out_ref[:, e, :] = result[:, e * FF : (e + 1) * FF]
 
-    for k in range(2):
-        send_x[k].wait_send()
-        send_g[k].wait_send()
+    for copy in (*tiles, send_x, *send_g):
+        copy.wait_send()
     for copy in mirrors.values():
         copy.wait_send()
     for copy in sends:
@@ -277,14 +322,16 @@
             pltpu.VMEM((2, 64, WIDE), jnp.float32),
             pltpu.VMEM((ZS, 32, WIDE), jnp.float32),
             pltpu.SemaphoreType.DMA((3,)),
-            pltpu.SemaphoreType.DMA((4,)),
-            pltpu.SemaphoreType.DMA((4,)),
             pltpu.SemaphoreType.DMA((8,)),
             pltpu.SemaphoreType.DMA((8,)),
-            pltpu.SemaphoreType.DMA((4, 2)),
-            pltpu.SemaphoreType.DMA((4, 2)),
-            pltpu.SemaphoreType.DMA((3, 2)),
-            pltpu.SemaphoreType.DMA((3, 2)),
+            pltpu.SemaphoreType.DMA((3,)),
+            pltpu.SemaphoreType.DMA((3,)),
+            pltpu.SemaphoreType.DMA((8, 4)),
+            pltpu.SemaphoreType.DMA((8, 4)),
+            pltpu.SemaphoreType.DMA((4, 4)),
+            pltpu.SemaphoreType.DMA((4, 4)),
+            pltpu.SemaphoreType.DMA((3, 4)),
+            pltpu.SemaphoreType.DMA((3, 4)),
             pltpu.SemaphoreType.DMA((2, 2)),
             pltpu.SemaphoreType.DMA((ZS,)),
         ],

time: 53.2 us -> 50.6 us (0.951)
  the two profiles are of different devices: /device:TPU:1 before, /device:TPU:9 now
where the time goes in v2:
time: 50.6 us; the launch traced here: 50.4 us
  Pallas kernels  47.2 us (93%)
  other arithmetic  2.45 us (5%)
  between operations  0.67 us (1%)
    pallas_call x1, Pallas kernels, per_device(): pl.pallas_call(kernel, out_shape=[jax.ShapeDtypeStruct((32, EXPERTS, FF),...  47.2 us
    broadcast_in_dim x1, other arithmetic, per_device(): step_direction[None]  1.69 us

profile of v2, /device:TPU:9, one launch (start us, length us, event | category | flops | bytes accessed | tf_op | source)
XLA Modules:
  0.0 50.4 jit_solution(3594845557940804092)
XLA Ops:
  0.6 0.0 copy-start.1
  0.6 0.0 copy-start
  0.7 47.2 %shard_map.93 = (f32[32,2,256]{2,1,0:T(2,128)}, f32[32,2,256]{2,1,0:T(2,128)}) custom-call(s32[2,3]{1,0:T(2,128)} %bitcast.26, s32[2,2]{1,0:T(2,128)} %bitcast.27, bf16[2,384,2048]{2,1,0:T(8,128)(2,1)} %bitcast.23, bf16[2,384,256]{2,1,0:T(8,128)(2,1)} %bitcast.24), custom_call_target="tpu_custom_call" | custom-call | tf_op jit(solution)/shard_map/pallas_call | solution.py:308
  47.9 0.0 copy-done.1
  47.9 0.0 copy-done
  47.9 1.7 %fusion.1 = (f32[1,32,2,256]{3,2,1,0:T(2,128)}, f32[32,2,256]{2,1,0:T(2,128)S(1)}) fusion(f32[1,32,2,256]{3,2,1,0:T(2,128)S(1)} %copy-done, f32[1,32,2,256]{3,2,1,0:T(2,128)S(1)} %copy-done.1, f32[32,2,256]{2,1,0:T(2,128)} %get-tuple-element.6, f32[32,2,256]{2,1,0:T(2,128)} %get-tuple-element.7), kind=kLoop, calls=%fused_computation.4 | loop fusion | flops 196608 | bytes 393216 | tf_op jit(solution)/shard_map/broadcast_in_dim | solution.py:353
  49.6 0.0 copy-start.2
  49.6 0.8 %fusion.3 = (f32[1,32,2,256]{3,2,1,0:T(2,128)}, f32[1,32,2,256]{3,2,1,0:T(2,128)}) fusion(f32[32,2,256]{2,1,0:T(2,128)S(1)} %get-tuple-element.9, f32[1,32,2,256]{3,2,1,0:T(2,128)S(1)} %copy-done.1, f32[1,32,2,256]{3,2,1,0:T(2,128)S(1)} %copy-done), kind=kLoop, calls=%fused_computation.6 | loop fusion | flops 114688 | bytes 327680 | tf_op jit(solution)/shard_map/broadcast_in_dim | solution.py:353
  50.4 0.0 copy-done.2
Async XLA Ops:
  0.6 47.3 %copy-start.1 = (f32[1,32,2,256]{3,2,1,0:T(2,128)S(1)}, f32[1,32,2,256]{3,2,1,0:T(2,128)}, u32[]{:S(2)}) copy-start(f32[1,32,2,256]{3,2,1,0:T(2,128)} %param.11) | copy-start | bytes 196612
  0.6 47.3 %copy-start = (f32[1,32,2,256]{3,2,1,0:T(2,128)S(1)}, f32[1,32,2,256]{3,2,1,0:T(2,128)}, u32[]{:S(2)}) copy-start(f32[1,32,2,256]{3,2,1,0:T(2,128)} %param.10) | copy-start | bytes 196612
  49.6 0.8 %copy-start.2 = (f32[32,2,256]{2,1,0:T(2,128)}, f32[32,2,256]{2,1,0:T(2,128)S(1)}, u32[]{:S(2)}) copy-start(f32[32,2,256]{2,1,0:T(2,128)S(1)} %get-tuple-element.9) | copy-start | bytes 196612

commit v3 on v2

--- a/solution.py
+++ b/solution.py
@@ -30,7 +30,7 @@
     be_ref, lc_ref, x_hbm, g_hbm, low_ref, high_ref,
     xb, graw, gb, total, mirror_out, mirror_in, ring_a, ring_b, last, zbuf,
     load_sem, tile_send, tile_recv, pair_send, pair_recv, mir_send, mir_recv,
-    a_send, a_recv, b_send, b_recv, z_send, z_recv,
+    a_send, a_recv, b_send, b_recv, z_send, z_recv, word_x, word_up, word_down,
 ):
     dp = lax.axis_index("dp")
     sec = lax.axis_index("section")
@@ -60,13 +60,49 @@
     loads[1].start()
     loads[0].start()
 
+    x_up = {"dp": dp, "section": (sec + 3) % 12}
+    x_down = {"dp": dp, "section": (sec + 9) % 12}
+    z_up = at(z + 1, y, core)
+    z_down = at(z - 1, y, core)
+
+    def signal(sem, device):
+        pl.semaphore_signal(sem, inc=1, device_id=device, device_id_type=MESH)
+
     barrier = pltpu.get_barrier_semaphore()
-    peers = [partner, mirror, next_a, next_b]
-    for dz in range(1, ZS):
-        for cc in range(2):
-            peers.append(at((z + dz) % ZS, y, cc))
+    peers = [partner, next_a, next_b, x_up, x_down]
     for peer in peers:
-        pl.semaphore_signal(barrier, inc=1, device_id=peer, device_id_type=MESH)
+        signal(barrier, peer)
+
+    @pl.when(z < ZS - 1)
+    def _():
+        signal(barrier, z_up)
+
+    @pl.when(z > 0)
+    def _():
+        signal(barrier, z_down)
+
+    n_peers = len(peers) + (z + 2) // 3 + (5 - z) // 3
+
+    def pass_word(step):
+        if step > 0:
+
+            @pl.when(z >= step)
+            def _():
+                pl.semaphore_wait(word_up.at[step - 1], 1)
+
+            @pl.when(z <= ZS - 1 - step)
+            def _():
+                pl.semaphore_wait(word_down.at[step - 1], 1)
+
+        if step < ZS - 1:
+
+            @pl.when(jnp.logical_and(z >= step, z < ZS - 1))
+            def _():
+                signal(word_up.at[step], z_up)
+
+            @pl.when(jnp.logical_and(z <= ZS - 1 - step, z > 0))
+            def _():
+                signal(word_down.at[step], z_down)
 
     def off(d):
         return (y + sgn * d + YS) % YS
@@ -105,9 +141,11 @@
                 kept = jnp.where(rows < limit, block, 0.0).astype(jnp.bfloat16)
                 gb[0, k, pl.ds(b * BLOCK, BLOCK), pl.ds(e * FF, FF)] = kept
 
-    pl.semaphore_wait(barrier, len(peers))
+    pl.semaphore_wait(barrier, n_peers)
     for copy in tiles[:2]:
         copy.start()
+    signal(word_x, x_up)
+    pass_word(0)
     load_g.wait()
     mask_direction(1)
     send_g[1].start()
@@ -179,6 +217,7 @@
     loads[1].wait()
     send_g[1].wait_recv()
     mirror_tiles(0, 1)
+    pl.semaphore_wait(word_x, 1)
     for t, k in pieces:
         send_mirror(4, t, k)
     mirror_tiles(1, 2)
@@ -232,6 +271,7 @@
     for t, k in pieces:
         add_mirror(4, t, k)
         hop(*ways[0], total.at[off(4), t, rows_of(k)], 0, t, k, next_a)
+    pass_word(1)
     mirror_tiles(3, 1)
     for t, k in pieces:
         send_mirror(1, t, k)
@@ -242,8 +282,10 @@
     for t, k in pieces:
         add_mirror(-3, t, k)
         hop(*ways[1], total.at[off(-3), t, rows_of(k)], 0, t, k, next_b)
+    pass_word(2)
     for t, k in pieces:
         forward_a(0, 3, t, k)
+    pass_word(3)
     for t, k in pieces:
         forward_a(1, 2, t, k)
         forward_b(0, -2, t, k)
@@ -334,6 +376,9 @@
             pltpu.SemaphoreType.DMA((3, 4)),
             pltpu.SemaphoreType.DMA((2, 2)),
             pltpu.SemaphoreType.DMA((ZS,)),
+            pltpu.SemaphoreType.REGULAR,
+            pltpu.SemaphoreType.REGULAR((ZS - 1,)),
+            pltpu.SemaphoreType.REGULAR((ZS - 1,)),
         ],
         compiler_params=pltpu.CompilerParams(
             collective_id=0, has_side_effects=True, vmem_limit_bytes=66700000

time: 50.6 us -> 48.5 us (0.958)
  the two profiles are of different devices: /device:TPU:9 before, /device:TPU:1 now
where the time goes in v3:
time: 48.5 us; the launch traced here: 48.3 us
  Pallas kernels  45.2 us (93%)
  other arithmetic  2.45 us (5%)
  between operations  0.67 us (1%)
    pallas_call x1, Pallas kernels, per_device(): pl.pallas_call(kernel, out_shape=[jax.ShapeDtypeStruct((32, EXPERTS, FF),...  45.2 us
    broadcast_in_dim x1, other arithmetic, per_device(): step_direction[None]  1.69 us

profile of v3, /device:TPU:1, one launch (start us, length us, event | category | flops | bytes accessed | tf_op | source)
XLA Modules:
  0.0 48.3 jit_solution(6542721674551631260)
XLA Ops:
  0.6 0.0 copy-start.1
  0.6 0.0 copy-start
  0.7 45.2 %shard_map.93 = (f32[32,2,256]{2,1,0:T(2,128)}, f32[32,2,256]{2,1,0:T(2,128)}) custom-call(s32[2,3]{1,0:T(2,128)} %bitcast.26, s32[2,2]{1,0:T(2,128)} %bitcast.27, bf16[2,384,2048]{2,1,0:T(8,128)(2,1)} %bitcast.23, bf16[2,384,256]{2,1,0:T(8,128)(2,1)} %bitcast.24), custom_call_target="tpu_custom_call" | custom-call | tf_op jit(solution)/shard_map/pallas_call | solution.py:350
  45.8 0.0 copy-done.1
  45.8 0.0 copy-done
  45.8 1.7 %fusion.1 = (f32[1,32,2,256]{3,2,1,0:T(2,128)}, f32[32,2,256]{2,1,0:T(2,128)S(1)}) fusion(f32[1,32,2,256]{3,2,1,0:T(2,128)S(1)} %copy-done, f32[1,32,2,256]{3,2,1,0:T(2,128)S(1)} %copy-done.1, f32[32,2,256]{2,1,0:T(2,128)} %get-tuple-element.6, f32[32,2,256]{2,1,0:T(2,128)} %get-tuple-element.7), kind=kLoop, calls=%fused_computation.4 | loop fusion | flops 196608 | bytes 393216 | tf_op jit(solution)/shard_map/broadcast_in_dim | solution.py:398
  47.5 0.0 copy-start.2
  47.5 0.8 %fusion.3 = (f32[1,32,2,256]{3,2,1,0:T(2,128)}, f32[1,32,2,256]{3,2,1,0:T(2,128)}) fusion(f32[32,2,256]{2,1,0:T(2,128)S(1)} %get-tuple-element.9, f32[1,32,2,256]{3,2,1,0:T(2,128)S(1)} %copy-done.1, f32[1,32,2,256]{3,2,1,0:T(2,128)S(1)} %copy-done), kind=kLoop, calls=%fused_computation.6 | loop fusion | flops 114688 | bytes 327680 | tf_op jit(solution)/shard_map/broadcast_in_dim | solution.py:398
  48.3 0.0 copy-done.2
Async XLA Ops:
  0.6 45.2 %copy-start.1 = (f32[1,32,2,256]{3,2,1,0:T(2,128)S(1)}, f32[1,32,2,256]{3,2,1,0:T(2,128)}, u32[]{:S(2)}) copy-start(f32[1,32,2,256]{3,2,1,0:T(2,128)} %param.11) | copy-start | bytes 196612
  0.6 45.2 %copy-start = (f32[1,32,2,256]{3,2,1,0:T(2,128)S(1)}, f32[1,32,2,256]{3,2,1,0:T(2,128)}, u32[]{:S(2)}) copy-start(f32[1,32,2,256]{3,2,1,0:T(2,128)} %param.10) | copy-start | bytes 196612
  47.5 0.8 %copy-start.2 = (f32[32,2,256]{2,1,0:T(2,128)}, f32[32,2,256]{2,1,0:T(2,128)S(1)}, u32[]{:S(2)}) copy-start(f32[32,2,256]{2,1,0:T(2,128)S(1)} %get-tuple-element.9) | copy-start | bytes 196612

commit v4 on v3

--- a/solution.py
+++ b/solution.py
@@ -27,7 +27,7 @@
 
 
 def kernel(
-    be_ref, lc_ref, x_hbm, g_hbm, low_ref, high_ref,
+    be_ref, lc_ref, x_hbm, g_hbm, out_ref,
     xb, graw, gb, total, mirror_out, mirror_in, ring_a, ring_b, last, zbuf,
     load_sem, tile_send, tile_recv, pair_send, pair_recv, mir_send, mir_recv,
     a_send, a_recv, b_send, b_recv, z_send, z_recv, word_x, word_up, word_down,
@@ -325,10 +325,9 @@
     def _():
         z_wait(z)
 
-    for i, out_ref in enumerate((low_ref, high_ref)):
-        result = zbuf[2 * i] + zbuf[2 * i + 1]
-        for e in range(EXPERTS):
-            out_ref[:, e, :] = result[:, e * FF : (e + 1) * FF]
+    result = (zbuf[0] + zbuf[1]) + (zbuf[2] + zbuf[3])
+    for e in range(EXPERTS):
+        out_ref[:, e, :] = result[:, e * FF : (e + 1) * FF]
 
     for copy in (*tiles, send_x, *send_g):
         copy.wait_send()
@@ -344,14 +343,24 @@
                 z_copy(t, k).wait_send()
 
 
+def update(sum_ref, one_ref, two_ref, grad_ref, first_ref, second_ref, step_ref):
+    grad_total = sum_ref[...]
+    new_first = beta_one * one_ref[...] + (1.0 - beta_one) * grad_total
+    new_second = beta_two * two_ref[...] + (1.0 - beta_two) * grad_total * grad_total
+    grad_ref[...] = grad_total
+    first_ref[...] = new_first
+    second_ref[...] = new_second
+    step_ref[...] = new_first / bias_first / (jnp.sqrt(new_second / bias_second) + adam_epsilon)
+
+
 def per_device(saved_inputs, hidden_grads, block_expert, live_counts, first_moment, second_moment):
     any_spec = pl.BlockSpec(memory_space=pl.ANY)
     smem_spec = pl.BlockSpec(memory_space=pltpu.SMEM)
-    low, high = pl.pallas_call(
+    summed = pl.pallas_call(
         kernel,
-        out_shape=[jax.ShapeDtypeStruct((32, EXPERTS, FF), jnp.float32)] * 2,
+        out_shape=jax.ShapeDtypeStruct((32, EXPERTS, FF), jnp.float32),
         in_specs=[smem_spec, smem_spec, any_spec, any_spec],
-        out_specs=[pl.BlockSpec(memory_space=pltpu.VMEM)] * 2,
+        out_specs=pl.BlockSpec(memory_space=pltpu.VMEM),
         scratch_shapes=[
             pltpu.VMEM((2, 2, ROWS, HALF), jnp.bfloat16),
             pltpu.VMEM((2, ROWS, FF), jnp.bfloat16),
@@ -389,13 +398,13 @@
         saved_inputs.reshape(2, ROWS, D),
         hidden_grads.reshape(2, ROWS, FF),
     )
-    grad_total = low + high
-    moment_one = first_moment[0]
-    moment_two = second_moment[0]
-    new_first = beta_one * moment_one + (1.0 - beta_one) * grad_total
-    new_second = beta_two * moment_two + (1.0 - beta_two) * grad_total * grad_total
-    step_direction = new_first / bias_first / (jnp.sqrt(new_second / bias_second) + adam_epsilon)
-    return (grad_total[None], new_first[None], new_second[None], step_direction[None])
+    outs = pl.pallas_call(
+        update,
+        out_shape=[jax.ShapeDtypeStruct((32, EXPERTS, FF), jnp.float32)] * 4,
+        in_specs=[pl.BlockSpec(memory_space=pltpu.VMEM)] * 3,
+        out_specs=[pl.BlockSpec(memory_space=pltpu.VMEM)] * 4,
+    )(summed, first_moment[0], second_moment[0])
+    return tuple(value[None] for value in outs)
 
 
 def solution(mesh):

time: 48.5 us -> 47.5 us (0.979)
  other arithmetic: 2.45 us -> 0 us
  Pallas kernels: 45.2 us -> 46.7 us
    broadcast_in_dim x2 -> x0, other arithmetic: 2.45 us -> none  [the longest x1 1.69 us: per_device(): step_direction[None]]
    pallas_call x1 -> x2, Pallas kernels: 45.2 us -> 46.7 us  [the longest x1 45 us: per_device(): pl.pallas_call(kernel, out_shape=jax.ShapeDtypeStruct((32, EXPERTS, FF),...]
where the time goes in v4:
time: 47.5 us; the launch traced here: 47.3 us
  Pallas kernels  46.7 us (98%)
  between operations  0.64 us (1%)
    pallas_call x1, Pallas kernels, per_device(): pl.pallas_call(kernel, out_shape=jax.ShapeDtypeStruct((32, EXPERTS, FF),...  45 us
    pallas_call x1, Pallas kernels, per_device(): pl.pallas_call(update, out_shape=[jax.ShapeDtypeStruct((32, EXPERTS, FF),...  1.68 us

profile of v4, /device:TPU:1, one launch (start us, length us, event | category | flops | bytes accessed | tf_op | source)
XLA Modules:
  0.0 47.3 jit_solution(3225023690690405201)
XLA Ops:
  0.6 45.0 %shard_map.93.sum_ref = f32[32,2,256]{2,1,0:T(2,128)} custom-call(s32[2,3]{1,0:T(2,128)} %bitcast.14, s32[2,2]{1,0:T(2,128)} %bitcast.15, bf16[2,384,2048]{2,1,0:T(8,128)(2,1)} %bitcast.10, bf16[2,384,256]{2,1,0:T(8,128)(2,1)} %bitcast.11), custom_call_target="tpu_custom_call" | custom-call | tf_op jit(solution)/shard_map/pallas_call | solution.py:359
  45.6 1.7 %shard_map.94 = (f32[32,2,256]{2,1,0:T(2,128)}, f32[32,2,256]{2,1,0:T(2,128)}, f32[32,2,256]{2,1,0:T(2,128)}, f32[32,2,256]{2,1,0:T(2,128)}) custom-call(f32[32,2,256]{2,1,0:T(2,128)} %shard_map.93.sum_ref, f32[32,2,256]{2,1,0:T(2,128)} %bitcast.12, f32[32,2,256]{2,1,0:T(2,128)} %bitcast.13), custom_call_target="tpu_custom_call" | custom-call | tf_op jit(solution)/shard_map/pallas_call | solution.py:401
